TPU v7x, 32 devices: a whole 2x2x4 slice. The times are simulated.
32 devices in a mesh: group: 2 (over x), ctx: 16 (over z, y, core).
Axes of the slice: x: 2, y: 2, z: 4, core: 2. Of those that a mesh axis runs over, the one named last changes fastest.
Arguments:
- queries: bfloat16 [256, 8, 8192], P(('group', 'ctx')), parts along dimension 0, may hold values from -40 to 40
- kv_cache: bfloat16 [32, 2, 512, 1024], P(('group', 'ctx')), parts along dimension 0, may hold values from -16 to 16
- page_counts: int32 [16], P('group'), parts along dimension 0, may hold values from 1 to 6, as said below
- doc_ids: int32 [16], P('group'), parts along dimension 0, may hold values from 0 to 7, each once
Outputs:
- attended: bfloat16 [256, 8, 8192], P(('group', 'ctx')), parts along dimension 0
There are 2 independent parts, one for each index of `group`. A program takes and returns all parts, laid end to end along the dimension named above; each array names one. Nothing has to cross between parts.
Inputs may be any that keep to these rules, and one draw needn't show every extreme that they name: `page_counts`: the counts sum to 16; every document holds at least 1 pages, some document exactly 1, and some document exactly 6. `doc_ids`: every document is named by exactly one question block.
All inputs are finite; a program needn't handle non-finite values.
Results may differ from a plain program's by a relative error of at most 0.0031.
Values may be sent and summed in bfloat16 or wider, within the bound.
A program may use at most 128 MiB of HBM per device.

v0:
```python
import functools

import jax
import jax.numpy as jnp
from jax import lax
from jax.experimental import pallas as pl
from jax.experimental.pallas import tpu as pltpu
from jax.sharding import PartitionSpec as P

HEAD_DIM = 128
CHUNKS = 4


def attend_kernel(
    peers, counts, doc_ids, q_hbm, kv_hbm, out_hbm,
    raw_buf, doc_buf, send_buf, q_buf, o_buf, got_buf, s_buf, stats_buf, w_buf, top_buf,
    run_buf, out_buf, kv_buf, ends, page_doc, page_block, fresh,
    raw_sem, q_send, q_recv, o_send, o_recv, s_send, s_recv, own_q_sem, own_o_sem, own_s_sem,
    kv_sem, out_sem,
):
    chunks, _, rows, wide = q_buf.shape
    blocks = counts.shape[0]
    me = lax.axis_index("ctx")
    tokens = peers * rows
    heads_chunk = wide // HEAD_DIM
    kv_heads = kv_buf.shape[2] // HEAD_DIM
    groups = chunks * heads_chunk // kv_heads
    mesh_id = pl.DeviceIdType.MESH

    barrier = pltpu.get_barrier_semaphore()

    @pl.loop(1, peers)
    def _(k):
        pl.semaphore_signal(
            barrier, inc=1, device_id={"ctx": lax.rem(me + k, peers)}, device_id_type=mesh_id
        )

    def columns(c):
        return pl.ds(c * wide, wide)

    raw_copies = [
        pltpu.make_async_copy(q_hbm.at[:, :, columns(c)], raw_buf.at[c], raw_sem.at[c])
        for c in range(chunks)
    ]
    for copy in raw_copies:
        copy.start()
    kv_copy = pltpu.make_async_copy(kv_hbm.at[0], kv_buf, kv_sem)
    kv_copy.start()

    end = 0
    for j in range(blocks):
        end = end + counts[j]
        ends[j] = end

    def locate(n, before):
        doc = 0
        for j in range(blocks):
            doc = doc + (n >= ends[j]).astype(jnp.int32)
        block = 0
        for j in range(1, blocks):
            block = block + jnp.where(doc_ids[j] == doc, j, 0)
        page_doc[n] = doc
        page_block[n] = block
        fresh[n] = (doc != before).astype(jnp.int32)
        return doc

    lax.fori_loop(0, peers, locate, jnp.int32(-1))
    fresh[peers] = 1

    def send(src, dst, send_sem, recv_sem):
        @pl.loop(1, peers)
        def _(k):
            peer = lax.rem(me + k, peers)
            pltpu.make_async_remote_copy(
                src_ref=src.at[peer], dst_ref=dst.at[me], send_sem=send_sem,
                recv_sem=recv_sem, device_id={"ctx": peer}, device_id_type=mesh_id,
            ).start()

    def drain(ref, sem):
        part = ref.at[pl.ds(0, peers - 1)]
        pltpu.make_async_copy(part, part, sem).wait()

    own_q, own_o = [], []
    for c in range(chunks):
        raw_copies[c].wait()
        raw = raw_buf[c].astype(jnp.float32)
        doc_buf[c] = jnp.swapaxes(raw, 0, 1).astype(jnp.bfloat16)

        @pl.loop(0, peers)
        def _(n):
            send_buf[c, n] = doc_buf[c, page_block[n]]

        if c == 0:
            pl.semaphore_wait(barrier, peers - 1)
        send(send_buf.at[c], q_buf.at[c], q_send.at[c], q_recv.at[c])
        copy = pltpu.make_async_copy(send_buf.at[c, me], q_buf.at[c, me], own_q_sem.at[c])
        copy.start()
        own_q.append(copy)

    s_buf[...] = jnp.zeros_like(s_buf)
    kv_copy.wait()
    lane = lax.broadcasted_iota(jnp.int32, (tokens, 128), 1)
    own_s = pltpu.make_async_copy(s_buf.at[me], stats_buf.at[me], own_s_sem)
    for c in range(chunks):
        own_q[c].wait()
        drain(q_buf.at[c], q_recv.at[c])

        def head(j, carry):
            lanes = pl.ds(pl.multiple_of(j * HEAD_DIM, HEAD_DIM), HEAD_DIM)
            h = c * heads_chunk + j
            kv_lanes = pl.ds(pl.multiple_of(h // groups * HEAD_DIM, HEAD_DIM), HEAD_DIM)
            q = q_buf[c, :, :, lanes].astype(jnp.float32).reshape(tokens, HEAD_DIM)
            s = lax.dot_general(
                q.astype(jnp.bfloat16), kv_buf[0, :, kv_lanes], (((1,), (1,)), ((), ())),
                preferred_element_type=jnp.float32,
            ) * HEAD_DIM ** (-0.5)
            top = jnp.max(s, axis=-1, keepdims=True)
            p = jnp.exp(s - top)
            total = jnp.sum(p, axis=-1, keepdims=True)
            o = jnp.dot(
                p.astype(jnp.bfloat16), kv_buf[1, :, kv_lanes],
                preferred_element_type=jnp.float32,
            ) / total
            o_buf[c, :, :, lanes] = o.reshape(peers, rows, HEAD_DIM).astype(jnp.bfloat16)
            old = s_buf[...].reshape(tokens, 128)
            new = jnp.where(lane == h, top, jnp.where(lane == h + 64, total, old))
            s_buf[...] = new.reshape(peers, rows, 128)
            return carry

        lax.fori_loop(0, heads_chunk, head, 0)
        if c == chunks - 1:
            send(s_buf, stats_buf, s_send, s_recv)
            own_s.start()
        send(o_buf.at[c], got_buf.at[c], o_send.at[c], o_recv.at[c])
        copy = pltpu.make_async_copy(o_buf.at[c, me], got_buf.at[c, me], own_o_sem.at[c])
        copy.start()
        own_o.append(copy)

    own_s.wait()
    drain(stats_buf, s_recv)

    def forward(n, top):
        mine = stats_buf[n]
        top = jnp.where(fresh[n] == 1, mine, jnp.maximum(top, mine))
        top_buf[n] = top
        return top

    def backward(i, top):
        n = peers - 1 - i
        top = jnp.where(fresh[n + 1] == 1, top_buf[n], top)
        top_buf[n] = top
        return top

    def weigh(n, total):
        mine = stats_buf[n]
        w = jnp.exp(mine - top_buf[n]) * pltpu.roll(mine, 128 - 64, 1)
        w_buf[n] = w
        total = jnp.where(fresh[n] == 1, w, total + w)
        top_buf[n] = total
        return total

    def norm(i, total):
        n = peers - 1 - i
        total = jnp.where(fresh[n + 1] == 1, top_buf[n], total)
        w_buf[n] = w_buf[n] / total
        return total

    zero = jnp.zeros((rows, 128), jnp.float32)
    lax.fori_loop(0, peers, forward, zero)
    lax.fori_loop(0, peers, backward, zero)
    lax.fori_loop(0, peers, weigh, zero)
    lax.fori_loop(0, peers, norm, zero)

    outs = []
    for c in range(chunks):
        own_o[c].wait()
        drain(got_buf.at[c], o_recv.at[c])

        def visit(n, acc):
            w = w_buf[n]
            w = jnp.concatenate(
                [
                    jnp.broadcast_to(w[:, h:h + 1], (rows, HEAD_DIM))
                    for h in range(c * heads_chunk, (c + 1) * heads_chunk)
                ],
                axis=1,
            )
            mine = w * got_buf[c, n].astype(jnp.float32)
            acc = jnp.where(fresh[n] == 1, mine, acc + mine)
            run_buf[n] = acc
            return acc

        lax.fori_loop(0, peers, visit, jnp.zeros((rows, wide), jnp.float32), unroll=2)
        picked = jnp.stack([run_buf[jnp.clip(ends[doc_ids[b]] - 1, 0, peers - 1)] for b in range(blocks)], axis=0)
        out_buf[c] = jnp.swapaxes(picked, 0, 1).astype(jnp.bfloat16)
        copy = pltpu.make_async_copy(out_buf.at[c], out_hbm.at[:, :, columns(c)], out_sem.at[c])
        copy.start()
        outs.append(copy)
    drain(s_buf, s_send)
    for c in range(chunks):
        drain(send_buf.at[c], q_send.at[c])
        drain(o_buf.at[c], o_send.at[c])
        outs[c].wait()


def body(queries, kv_cache, page_counts, doc_ids):
    peers = lax.axis_size("ctx")
    rows, blocks, width = queries.shape
    assert kv_cache.shape[0] == 1 and width == 64 * HEAD_DIM
    wide = width // CHUNKS
    any_spec = pl.BlockSpec(memory_space=pl.ANY)
    smem_spec = pl.BlockSpec(memory_space=pltpu.SMEM)
    dma = pltpu.SemaphoreType.DMA
    pieces = pltpu.VMEM((CHUNKS, peers, rows, wide), jnp.bfloat16)
    stats = pltpu.VMEM((peers, rows, 128), jnp.float32)
    return pl.pallas_call(
        functools.partial(attend_kernel, peers),
        out_shape=jax.ShapeDtypeStruct(queries.shape, jnp.bfloat16),
        in_specs=[smem_spec, smem_spec, any_spec, any_spec],
        out_specs=any_spec,
        scratch_shapes=[
            pltpu.VMEM((CHUNKS, rows, blocks, wide), jnp.bfloat16),
            pltpu.VMEM((CHUNKS, blocks, rows, wide), jnp.bfloat16),
            pieces, pieces, pieces, pieces,
            stats, stats, stats, stats,
            pltpu.VMEM((peers, rows, wide), jnp.float32),
            pltpu.VMEM((CHUNKS, rows, blocks, wide), jnp.bfloat16),
            pltpu.VMEM(kv_cache.shape[1:], jnp.bfloat16),
            pltpu.SMEM((blocks,), jnp.int32),
            pltpu.SMEM((peers,), jnp.int32),
            pltpu.SMEM((peers,), jnp.int32),
            pltpu.SMEM((peers + 1,), jnp.int32),
            dma((CHUNKS,)),
            dma((CHUNKS,)), dma((CHUNKS,)), dma((CHUNKS,)), dma((CHUNKS,)),
            dma(()), dma(()), dma((CHUNKS,)), dma((CHUNKS,)), dma(()),
            dma(()), dma((CHUNKS,)),
        ],
        compiler_params=pltpu.CompilerParams(collective_id=0, has_side_effects=True),
    )(page_counts, doc_ids, queries, kv_cache)


def solution(mesh):
    placed = (
        P(("group", "ctx"), None, None),
        P(("group", "ctx"), None, None, None),
        P("group"),
        P("group"),
    )
    return jax.shard_map(
        body, mesh=mesh, in_specs=placed, out_specs=P(("group", "ctx"), None, None), check_vma=False
    )
```

profile of v0, /device:TPU:0, one launch (start us, length us, event | category | flops | bytes accessed | tf_op | source)
XLA Modules:
  0.0 103.4 jit_solution(10026708081868214510)
XLA Ops:
  0.0 101.1 %shard_map.46 = bf16[8,8,8192]{2,1,0:T(8,128)(2,1)} custom-call(s32[8]{0:T(128)} %counts.1, s32[8]{0:T(128)} %doc_ids.1, bf16[8,8,8192]{2,1,0:T(8,128)(2,1)} %q_hbm.1, bf16[1,2,512,1024]{3,2,1,0:T(8,128)(2,1)} %kv_hbm.1), custom_call_target="tpu_custom_call" | custom-call | tf_op jit(solution)/shard_map/pallas_call | solution.py:216
  101.2 2.3 %copy.6 = bf16[8,8,8192]{2,1,0:T(8,128)(2,1)} copy(bf16[8,8,8192]{2,1,0:T(8,128)(2,1)} %shard_map.46) | data formatting | bytes 2097152
where the time goes:
time: 104 us; the launch traced here: 103 us
  Pallas kernels  101 us (97%)
  local copies, waits for them, and re-layouts  2.26 us (2%)
    pallas_call x1, Pallas kernels, body(): pl.pallas_call(functools.partial(attend_kernel, peers), out_shape=jax.Sha...  101 us
    unnamed x1, local copies, waits for them, and re-layouts  2.26 us

commit v1 on v0

--- a/solution.py
+++ b/solution.py
@@ -203,9 +203,436 @@
         outs[c].wait()
 
 
+STEPS = 16
+LAG = 4
+GROUPS = 4
+FAR = -1e30
+
+
+def merge(o1, l1, o2, l2):
+    top = jnp.maximum(l1, l2)
+    w1, w2 = jnp.exp(l1 - top), jnp.exp(l2 - top)
+    out = (w1 * o1.astype(jnp.float32) + w2 * o2.astype(jnp.float32)) / (w1 + w2)
+    return out.astype(jnp.bfloat16)
+
+
+def join(l1, l2):
+    top = jnp.maximum(l1, l2)
+    return top + jnp.log(jnp.exp(l1 - top) + jnp.exp(l2 - top))
+
+
+def to_row(col, first):
+    shape = (col.shape[0], 128)
+    hit = lax.broadcasted_iota(jnp.int32, shape, 1) == lax.broadcasted_iota(jnp.int32, shape, 0) + first
+    return jnp.sum(jnp.where(hit, col, 0.0), axis=0, keepdims=True)
+
+
+def to_col(row, first, count):
+    shape = (count, 128)
+    hit = lax.broadcasted_iota(jnp.int32, shape, 1) == lax.broadcasted_iota(jnp.int32, shape, 0) + first
+    return jnp.sum(jnp.where(hit, row, 0.0), axis=1, keepdims=True)
+
+
+def pick(parts, index):
+    got = parts[0]
+    for n in range(1, len(parts)):
+        got = jnp.where(index == n, parts[n], got)
+    return got
+
+
+def line_kernel(
+    counts, doc_ids, q_hbm, kv_hbm, out_hbm,
+    raw, kv, blk, s1r, xs, xr, xls, xlr, cs, cr, dr, dlr, fs, fr, fls, flr,
+    qt, run, lse, oh, lh, fin, ends,
+    q_ssem, q_rsem, q_own, kv_ssem, kv_rsem, kv_own, s_ssem, s_rsem, x_ssem, x_rsem, xl_ssem, xl_rsem,
+    c_ssem, c_rsem, d_ssem, d_rsem, dl_ssem, dl_rsem, f_ssem, f_rsem, fl_ssem, fl_rsem,
+    o_ssem, o_rsem, o_own,
+):
+    blocks = counts.shape[0]
+    rounds = STEPS + LAG
+    me = lax.axis_index("ctx")
+    z, mine = me // 4, me % 4
+    upper = z // 2
+    hub = (z == 1) | (z == 2)
+    leaf = (z == 0) | (z == 3)
+    away = jnp.where((z == 0) | (z == 2), me + 4, me - 4)
+    across = jnp.where(z == 1, me + 4, me - 4)
+    mesh_id = pl.DeviceIdType.MESH
+
+    def plane(k):
+        return z * 4 + (mine + k) % 4, (mine + k) % 4
+
+    barrier = pltpu.get_barrier_semaphore()
+    for k in range(1, 4):
+        pl.semaphore_signal(barrier, inc=1, device_id={"ctx": plane(k)[0]}, device_id_type=mesh_id)
+    pl.semaphore_signal(barrier, inc=1, device_id={"ctx": away}, device_id_type=mesh_id)
+
+    @pl.when(hub)
+    def _():
+        pl.semaphore_signal(barrier, inc=1, device_id={"ctx": across}, device_id_type=mesh_id)
+
+    def lanes(i, g):
+        return pl.ds(pl.multiple_of(i * 2048 + g * 512, 128), 512)
+
+    def heads(i, h):
+        return pl.ds(pl.multiple_of(i * 256 + h * 128, 128), 128)
+
+    own = []
+    for g in range(GROUPS):
+        own.append(pltpu.make_async_copy(q_hbm.at[:, :, lanes(mine, g)], raw.at[g, mine], q_own.at[g]))
+    for h in range(2):
+        own.append(pltpu.make_async_copy(kv_hbm.at[0, :, :, heads(mine, h)], kv.at[h, mine], kv_own.at[h]))
+    for copy in own:
+        copy.start()
+
+    def remote(src, dst, ssem, rsem, peer):
+        pltpu.make_async_remote_copy(
+            src_ref=src, dst_ref=dst, send_sem=ssem, recv_sem=rsem,
+            device_id={"ctx": peer}, device_id_type=mesh_id,
+        ).start()
+
+    def wait(ref, sem):
+        pltpu.make_async_copy(ref, ref, sem).wait()
+
+    @pl.when(hub)
+    def _():
+        pl.semaphore_wait(barrier, 5)
+
+    @pl.when(leaf)
+    def _():
+        pl.semaphore_wait(barrier, 4)
+
+    def send_group(g):
+        for k in range(1, 4):
+            peer, i = plane(k)
+            remote(q_hbm.at[:, :, lanes(i, g)], raw.at[g, mine], q_ssem, q_rsem.at[g], peer)
+
+    def send_kv(h):
+        for k in range(1, 4):
+            peer, i = plane(k)
+            remote(kv_hbm.at[0, :, :, heads(i, h)], kv.at[h, mine], kv_ssem, kv_rsem.at[h], peer)
+
+    send_group(0)
+    send_kv(0)
+    send_group(1)
+    send_group(2)
+    send_group(3)
+    send_kv(1)
+
+    end = 0
+    for j in range(blocks):
+        end = end + counts[j]
+        ends[j] = end
+
+    def doc_at(n):
+        doc = 0
+        for j in range(blocks):
+            doc = doc + (n >= ends[j]).astype(jnp.int32)
+        return doc
+
+    def block_at(n):
+        doc = doc_at(n)
+        block = 0
+        for j in range(1, blocks):
+            block = block + jnp.where(doc_ids[j] == doc, j, 0)
+        return block
+
+    stop = [ends[doc_ids[b]] for b in range(blocks)]
+    start = [stop[b] - counts[doc_ids[b]] for b in range(blocks)]
+
+    def has(b, first):
+        return (start[b] < first + 4) & (stop[b] > first)
+
+    def last(b, first):
+        return jnp.clip(stop[b] - 1 - first, 0, 3)
+
+    first = 4 * z
+    rim = jnp.where(upper == 0, 0, 12)
+    other = [jnp.where(upper == 0, (stop[b] > 8).astype(jnp.int32), (start[b] < 8).astype(jnp.int32)) == 1 for b in range(blocks)]
+    page_block = [block_at(first + p) for p in range(4)]
+    same = [None] + [doc_at(first + p) == doc_at(first + p - 1) for p in range(1, 4)]
+    seam = jnp.where(upper == 0, 3, 11)
+    seam_block = block_at(seam)
+    seam_cut = doc_at(seam) == doc_at(seam + 1)
+    mid_block = block_at(7)
+    mid_cut = doc_at(7) == doc_at(8)
+
+    def of(values, index):
+        got = values[0]
+        for n in range(1, blocks):
+            got = jnp.where(index == n, values[n], got)
+        return got
+
+    def has_at(b, base):
+        return (of(start, b) < base + 4) & (of(stop, b) > base)
+
+    def last_at(b, base):
+        return jnp.clip(of(stop, b) - 1 - base, 0, 3)
+
+    def prepare(g):
+        for n in range(GROUPS):
+            @pl.when(g == n)
+            def _():
+                own[n].wait()
+        part = raw.at[g, pl.ds(0, 3)]
+        wait(part, q_rsem.at[g])
+        value = raw[g].astype(jnp.float32).reshape(32, blocks, 512)
+        value = jnp.swapaxes(value, 0, 1).astype(jnp.bfloat16)
+        for n in range(4):
+            blk[g * 4 + n] = value[:, :, n * 128:(n + 1) * 128]
+
+    def wait_kv(v):
+        for h in range(2):
+            @pl.when(v == h * (STEPS // 2))
+            def _():
+                own[GROUPS + h].wait()
+                wait(kv.at[h, pl.ds(0, 3)], kv_rsem.at[h])
+
+    sub = lax.broadcasted_iota(jnp.int32, (8, 128), 0)
+
+    def attend(v, question):
+        h = v // (STEPS // 2)
+        tile = jnp.zeros((8, 128), jnp.float32)
+        top = total = mixed = None
+        for p in range(4):
+            s = lax.dot_general(
+                question(p), kv[h, p, 0], (((1,), (1,)), ((), ())),
+                preferred_element_type=jnp.float32,
+            ) * HEAD_DIM ** (-0.5)
+            t = jnp.max(s, axis=-1, keepdims=True)
+            e = jnp.exp(s - t)
+            n = jnp.sum(e, axis=-1, keepdims=True)
+            o = jnp.dot(e.astype(jnp.bfloat16), kv[h, p, 1], preferred_element_type=jnp.float32)
+            if p == 0:
+                top, total, mixed = t, n, o
+            else:
+                before = jnp.where(same[p], top, FAR)
+                top = jnp.maximum(before, t)
+                a, b = jnp.exp(before - top), jnp.exp(t - top)
+                total = a * total + b * n
+                mixed = a * mixed + b * o
+            run[v, p] = (mixed / total).astype(jnp.bfloat16)
+            tile = jnp.where(sub == p, to_row(top + jnp.log(total), 0), tile)
+        lse[v] = tile
+
+    def finish(u, values):
+        value = jnp.stack([x.astype(jnp.float32) for x in values], axis=0)
+        fin[u] = jnp.swapaxes(value, 0, 1).astype(jnp.bfloat16)
+        column = pl.ds(pl.multiple_of(mine * 2048 + u * 128, 128), 128)
+        for k in range(1, 4):
+            peer, i = plane(k)
+            remote(fin.at[u, pl.ds(i * 8, 8)], out_hbm.at[:, :, column], o_ssem, o_rsem, peer)
+        pltpu.make_async_copy(fin.at[u, pl.ds(mine * 8, 8)], out_hbm.at[:, :, column], o_own).start()
+
+    @pl.when(leaf)
+    def _():
+        def pass_on(g):
+            prepare(g)
+            for n in range(4):
+                c = g * 4 + n
+                remote(blk.at[c], s1r.at[c], s_ssem, s_rsem.at[c], away)
+
+        pass_on(0)
+        has_own = [has(b, first) for b in range(blocks)]
+        last_own = [last(b, first) for b in range(blocks)]
+        seam_last = last_at(seam_block, first)
+
+        @pl.loop(0, STEPS + LAG + 1)
+        def _(t):
+            @pl.when((t % 4 == 0) & (t < STEPS - 4))
+            def _():
+                pass_on(t // 4 + 1)
+
+            @pl.when(t < STEPS)
+            def _():
+                wait_kv(t)
+                wait(cr.at[t], c_rsem.at[t])
+                attend(t, lambda p: jnp.concatenate([blk[t, page_block[p]], cr[t, p]], axis=0))
+                remote(run.at[t, :, pl.ds(32, 96)], dr.at[t], d_ssem, d_rsem.at[t], away)
+                remote(lse.at[t], dlr.at[t], dl_ssem, dl_rsem.at[t], away)
+
+            @pl.when(t >= LAG + 1)
+            def _():
+                u = t - LAG - 1
+                wait(fr.at[u], f_rsem.at[u])
+                wait(flr.at[u], fl_rsem.at[u])
+                near = to_col(pick([lse[u, p:p + 1] for p in range(4)], seam_last), 0, 32)
+                far = to_col(flr[u, 0:1], 0, 32)
+                whole = merge(
+                    run[u, seam_last, 0:32], near,
+                    of([fr[u, b] for b in range(blocks)], seam_block), far,
+                )
+                values = []
+                for b in range(blocks):
+                    value = jnp.where(has_own[b], run[u, last_own[b], 0:32], fr[u, b])
+                    values.append(jnp.where(seam_cut & (seam_block == b), whole, value))
+                finish(u, values)
+
+        wait(blk, s_ssem)
+        wait(dr, d_ssem)
+        wait(dlr, dl_ssem)
+
+    @pl.when(hub)
+    def _():
+        prepare(jnp.int32(0))
+        has_rim = [has(b, rim) for b in range(blocks)]
+        last_rim = [last(b, rim) for b in range(blocks)]
+        has_own = [has(b, first) for b in range(blocks)]
+        last_own = [last(b, first) for b in range(blocks)]
+        rim_block = [block_at(rim + p) for p in range(4)]
+        seam_rim, seam_own = last_at(seam_block, rim), last_at(seam_block, first)
+        mid_rim, mid_own = last_at(mid_block, rim), last_at(mid_block, first)
+        mid_has_rim = has_at(mid_block, rim)
+        lane = lax.broadcasted_iota(jnp.int32, (1, 128), 1)
+
+        def rows(ref, u):
+            return [ref[u, p:p + 1] for p in range(4)]
+
+        @pl.loop(0, rounds + 1)
+        def _(t):
+            @pl.when((t >= LAG) & (t < rounds))
+            def _():
+                w = t - LAG
+                wait(dr.at[w], d_rsem.at[w])
+                wait(dlr.at[w], dl_rsem.at[w])
+                rim_o = [dr[w, p] for p in range(4)]
+                whole = merge(
+                    pick(rim_o, seam_rim), to_col(pick(rows(dlr, w), seam_rim), 32, 96),
+                    run[w, seam_own, 32:128], to_col(pick(rows(lse, w), seam_own), 32, 96),
+                )
+                for b in range(blocks):
+                    value = jnp.where(has_own[b], run[w, last_own[b], 32:128], pick(rim_o, last_rim[b]))
+                    oh[w, b] = jnp.where(seam_cut & (seam_block == b), whole, value)
+                near = pick(rows(lse, w), mid_own)
+                far = jnp.where(mid_has_rim, pick(rows(dlr, w), mid_rim), FAR)
+                lh[w] = jnp.broadcast_to(join(near, far), (8, 128))
+
+            @pl.when(t < rounds)
+            def _():
+                w = jnp.maximum(t - LAG, 0)
+                c = jnp.minimum(t, STEPS - 1)
+
+                @pl.when((t % 4 == 0) & (t > 0) & (t < STEPS))
+                def _():
+                    prepare(t // 4)
+
+                @pl.when(t < STEPS)
+                def _():
+                    wait(s1r.at[t], s_rsem.at[t])
+
+                asks = t < STEPS
+                for b in range(blocks):
+                    ask = other[b] & asks
+                    xs[t, b, 0:32] = jnp.where(ask, s1r[c, b], oh[w, b, 32:64])
+                    xs[t, b, 32:64] = jnp.where(ask, blk[c, b], oh[w, b, 64:96])
+                xs[t, blocks] = oh[w, mid_block, 32:96]
+                xls[t] = lh[w]
+                remote(xs.at[t], xr.at[t], x_ssem, x_rsem.at[t], across)
+                remote(xls.at[t], xlr.at[t], xl_ssem, xl_rsem.at[t], across)
+
+            @pl.when(t >= 1)
+            def _():
+                v = t - 1
+                wait(xr.at[v], x_rsem.at[v])
+                wait(xlr.at[v], xl_rsem.at[v])
+
+                @pl.when(v < STEPS)
+                def _():
+                    for b in range(blocks):
+                        qt[v, b, 0:32] = s1r[v, b]
+                        qt[v, b, 32:64] = blk[v, b]
+                        qt[v, b, 64:128] = xr[v, b]
+                    for p in range(4):
+                        cs[v, p] = qt[v, rim_block[p], 32:128]
+                    remote(cs.at[v], cr.at[v], c_ssem, c_rsem.at[v], away)
+
+                @pl.when(v >= LAG)
+                def _():
+                    u = v - LAG
+                    near = jnp.where(lane < 32, pick(rows(lse, u), mid_own), lh[u, 0:1])
+                    far = pltpu.roll(xlr[v, 0:1], 64, 1)
+                    part = jnp.concatenate([run[u, mid_own, 0:32], oh[u, mid_block, 0:32]], axis=0)
+                    whole = merge(part, to_col(near, 0, 64), xr[v, blocks], to_col(far, 0, 64))
+                    values = []
+                    for b in range(blocks):
+                        cut = mid_cut & (mid_block == b)
+                        leafs = jnp.where(other[b], xr[v, b, 0:32], run[u, last_own[b], 0:32])
+                        hubs = jnp.where(other[b], xr[v, b, 32:64], oh[u, b, 0:32])
+                        fs[u, b] = jnp.where(cut, whole[0:32], leafs)
+                        values.append(jnp.where(cut, whole[32:64], hubs))
+                    tail = pick(rows(lse, u), seam_own)
+                    tail = jnp.where(mid_cut & (mid_block == seam_block), join(tail, far), tail)
+                    fls[u] = jnp.broadcast_to(tail, (8, 128))
+                    remote(fs.at[u], fr.at[u], f_ssem, f_rsem.at[u], away)
+                    remote(fls.at[u], flr.at[u], fl_ssem, fl_rsem.at[u], away)
+                    finish(u, values)
+
+            @pl.when((t >= LAG - 1) & (t < STEPS + LAG - 1))
+            def _():
+                v = t - LAG + 1
+                wait_kv(v)
+                attend(v, lambda p: qt[v, page_block[p]])
+
+        wait(xs, x_ssem)
+        wait(xls, xl_ssem)
+        wait(cs, c_ssem)
+        wait(fs, f_ssem)
+        wait(fls, fl_ssem)
+
+    for g in range(GROUPS):
+        wait(raw.at[g, pl.ds(0, 3)], q_ssem)
+    for h in range(2):
+        wait(kv.at[h, pl.ds(0, 3)], kv_ssem)
+    theirs, ours = fin.at[:, pl.ds(0, 24)], fin.at[:, pl.ds(0, 8)]
+    wait(theirs, o_ssem)
+    wait(theirs, o_rsem)
+    wait(ours, o_own)
+
+
+def line_call(queries, kv_cache, page_counts, doc_ids):
+    blocks = queries.shape[1]
+    bf16, f32 = jnp.bfloat16, jnp.float32
+    any_spec = pl.BlockSpec(memory_space=pl.ANY)
+    smem_spec = pl.BlockSpec(memory_space=pltpu.SMEM)
+    dma = pltpu.SemaphoreType.DMA
+    rounds = STEPS + LAG
+    tiles = pltpu.VMEM((STEPS, 8, 128), f32)
+    mids = pltpu.VMEM((rounds, 8, 128), f32)
+    pieces = pltpu.VMEM((STEPS, blocks, 32, 128), bf16)
+    swaps = pltpu.VMEM((rounds, blocks + 1, 64, 128), bf16)
+    quads = pltpu.VMEM((STEPS, 4, 96, 128), bf16)
+    one, step, mid = dma(()), dma((STEPS,)), dma((rounds,))
+    return pl.pallas_call(
+        line_kernel,
+        out_shape=jax.ShapeDtypeStruct(queries.shape, bf16),
+        in_specs=[smem_spec, smem_spec, any_spec, any_spec],
+        out_specs=any_spec,
+        scratch_shapes=[
+            pltpu.VMEM((GROUPS, 4, 8, blocks, 512), bf16),
+            pltpu.VMEM((2, 4, 2, 512, 128), bf16),
+            pieces, pieces, swaps, swaps, mids, mids,
+            quads, quads, quads, tiles, pieces, pieces, tiles, tiles,
+            pltpu.VMEM((STEPS, blocks, 128, 128), bf16),
+            pltpu.VMEM((STEPS, 4, 128, 128), bf16),
+            tiles,
+            pltpu.VMEM((STEPS, blocks, 96, 128), bf16),
+            tiles,
+            pltpu.VMEM((STEPS, 32, blocks, 128), bf16),
+            pltpu.SMEM((blocks,), jnp.int32),
+            one, dma((GROUPS,)), dma((GROUPS,)), one, dma((2,)), dma((2,)),
+            one, step, one, mid, one, mid,
+            one, step, one, step, one, step, one, step, one, step,
+            one, one, one,
+        ],
+        compiler_params=pltpu.CompilerParams(collective_id=1, has_side_effects=True),
+    )(page_counts, doc_ids, queries, kv_cache)
+
+
 def body(queries, kv_cache, page_counts, doc_ids):
     peers = lax.axis_size("ctx")
     rows, blocks, width = queries.shape
+    if (peers, rows, blocks) == (16, 8, 8) and kv_cache.shape == (1, 2, 512, 1024):
+        return line_call(queries, kv_cache, page_counts, doc_ids)
     assert kv_cache.shape[0] == 1 and width == 64 * HEAD_DIM
     wide = width // CHUNKS
     any_spec = pl.BlockSpec(memory_space=pl.ANY)

time: 104 us -> 110 us (1.058)
  Pallas kernels: 101 us -> 107 us
    pallas_call x1, Pallas kernels: 101 us -> 107 us  [line_call(): pl.pallas_call(line_kernel, out_shape=jax.ShapeDtypeStruct(queries.shape,...]
where the time goes in v1:
time: 110 us
  Pallas kernels  107 us (97%)
  local copies, waits for them, and re-layouts  2.26 us (2%)
    pallas_call x1, Pallas kernels, line_call(): pl.pallas_call(line_kernel, out_shape=jax.ShapeDtypeStruct(queries.shape,...  107 us
    unnamed x1, local copies, waits for them, and re-layouts  2.26 us

profile of v1, /device:TPU:0, one launch (start us, length us, event | category | flops | bytes accessed | tf_op | source)
XLA Modules:
  0.0 109.5 jit_solution(6135371260726117976)
XLA Ops:
  0.0 107.2 %shard_map.46 = bf16[8,8,8192]{2,1,0:T(8,128)(2,1)} custom-call(s32[8]{0:T(128)} %counts.1, s32[8]{0:T(128)} %doc_ids.1, bf16[8,8,8192]{2,1,0:T(8,128)(2,1)} %q_hbm.1, bf16[1,2,512,1024]{3,2,1,0:T(8,128)(2,1)} %kv_hbm.1), custom_call_target="tpu_custom_call" | custom-call | tf_op jit(solution)/shard_map/pallas_call | solution.py:605
  107.2 2.3 %copy.6 = bf16[8,8,8192]{2,1,0:T(8,128)(2,1)} copy(bf16[8,8,8192]{2,1,0:T(8,128)(2,1)} %shard_map.46) | data formatting | bytes 2097152

commit v2 on v1

--- a/solution.py
+++ b/solution.py
@@ -204,8 +204,10 @@
 
 
 STEPS = 16
-LAG = 4
-GROUPS = 4
+LAG = 6
+BACK = 2
+GROUPS = 8
+AHEAD = 4
 FAR = -1e30
 
 
@@ -243,7 +245,7 @@
 def line_kernel(
     counts, doc_ids, q_hbm, kv_hbm, out_hbm,
     raw, kv, blk, s1r, xs, xr, xls, xlr, cs, cr, dr, dlr, fs, fr, fls, flr,
-    qt, run, lse, oh, lh, fin, ends,
+    qt, run, lse, oh, lh, fin, turn, done, ends,
     q_ssem, q_rsem, q_own, kv_ssem, kv_rsem, kv_own, s_ssem, s_rsem, x_ssem, x_rsem, xl_ssem, xl_rsem,
     c_ssem, c_rsem, d_ssem, d_rsem, dl_ssem, dl_rsem, f_ssem, f_rsem, fl_ssem, fl_rsem,
     o_ssem, o_rsem, o_own,
@@ -272,18 +274,15 @@
         pl.semaphore_signal(barrier, inc=1, device_id={"ctx": across}, device_id_type=mesh_id)
 
     def lanes(i, g):
-        return pl.ds(pl.multiple_of(i * 2048 + g * 512, 128), 512)
+        return pl.ds(pl.multiple_of(i * 2048 + g * 256, 128), 256)
 
     def heads(i, h):
         return pl.ds(pl.multiple_of(i * 256 + h * 128, 128), 128)
 
-    own = []
     for g in range(GROUPS):
-        own.append(pltpu.make_async_copy(q_hbm.at[:, :, lanes(mine, g)], raw.at[g, mine], q_own.at[g]))
+        pltpu.make_async_copy(q_hbm.at[:, :, lanes(mine, g)], raw.at[g, mine], q_own.at[g]).start()
     for h in range(2):
-        own.append(pltpu.make_async_copy(kv_hbm.at[0, :, :, heads(mine, h)], kv.at[h, mine], kv_own.at[h]))
-    for copy in own:
-        copy.start()
+        pltpu.make_async_copy(kv_hbm.at[0, :, :, heads(mine, h)], kv.at[h, mine], kv_own.at[h]).start()
 
     def remote(src, dst, ssem, rsem, peer):
         pltpu.make_async_remote_copy(
@@ -312,11 +311,11 @@
             peer, i = plane(k)
             remote(kv_hbm.at[0, :, :, heads(i, h)], kv.at[h, mine], kv_ssem, kv_rsem.at[h], peer)
 
-    send_group(0)
+    for g in range(AHEAD):
+        send_group(g)
     send_kv(0)
-    send_group(1)
-    send_group(2)
-    send_group(3)
+    for g in range(AHEAD, GROUPS):
+        send_group(g)
     send_kv(1)
 
     end = 0
@@ -328,64 +327,54 @@
         doc = 0
         for j in range(blocks):
             doc = doc + (n >= ends[j]).astype(jnp.int32)
-        return doc
-
-    def block_at(n):
-        doc = doc_at(n)
+        return jnp.minimum(doc, blocks - 1)
+
+    stop = [ends[j] for j in range(blocks)]
+    start = [stop[j] - counts[j] for j in range(blocks)]
+    doc_block = []
+    for j in range(blocks):
         block = 0
-        for j in range(1, blocks):
-            block = block + jnp.where(doc_ids[j] == doc, j, 0)
-        return block
-
-    stop = [ends[doc_ids[b]] for b in range(blocks)]
-    start = [stop[b] - counts[doc_ids[b]] for b in range(blocks)]
-
-    def has(b, first):
-        return (start[b] < first + 4) & (stop[b] > first)
-
-    def last(b, first):
-        return jnp.clip(stop[b] - 1 - first, 0, 3)
+        for b in range(1, blocks):
+            block = block + jnp.where(doc_ids[b] == j, b, 0)
+        doc_block.append(jnp.minimum(block, blocks - 1))
+
+    def has(j, first):
+        return (start[j] < first + 4) & (stop[j] > first)
+
+    def last(j, first):
+        return jnp.clip(stop[j] - 1 - first, 0, 3)
+
+    def has_at(j, first):
+        return (ends[j] - counts[j] < first + 4) & (ends[j] > first)
+
+    def last_at(j, first):
+        return jnp.clip(ends[j] - 1 - first, 0, 3)
 
     first = 4 * z
     rim = jnp.where(upper == 0, 0, 12)
-    other = [jnp.where(upper == 0, (stop[b] > 8).astype(jnp.int32), (start[b] < 8).astype(jnp.int32)) == 1 for b in range(blocks)]
-    page_block = [block_at(first + p) for p in range(4)]
-    same = [None] + [doc_at(first + p) == doc_at(first + p - 1) for p in range(1, 4)]
+    other = [jnp.where(upper == 0, (stop[j] > 8).astype(jnp.int32), (start[j] < 8).astype(jnp.int32)) == 1 for j in range(blocks)]
+    page_doc = [doc_at(first + p) for p in range(4)]
+    same = [None] + [page_doc[p] == page_doc[p - 1] for p in range(1, 4)]
     seam = jnp.where(upper == 0, 3, 11)
-    seam_block = block_at(seam)
-    seam_cut = doc_at(seam) == doc_at(seam + 1)
-    mid_block = block_at(7)
-    mid_cut = doc_at(7) == doc_at(8)
-
-    def of(values, index):
-        got = values[0]
-        for n in range(1, blocks):
-            got = jnp.where(index == n, values[n], got)
-        return got
-
-    def has_at(b, base):
-        return (of(start, b) < base + 4) & (of(stop, b) > base)
-
-    def last_at(b, base):
-        return jnp.clip(of(stop, b) - 1 - base, 0, 3)
+    seam_doc, mid_doc = doc_at(seam), doc_at(7)
+    seam_cut = seam_doc == doc_at(seam + 1)
+    mid_cut = mid_doc == doc_at(8)
 
     def prepare(g):
-        for n in range(GROUPS):
-            @pl.when(g == n)
-            def _():
-                own[n].wait()
-        part = raw.at[g, pl.ds(0, 3)]
-        wait(part, q_rsem.at[g])
-        value = raw[g].astype(jnp.float32).reshape(32, blocks, 512)
-        value = jnp.swapaxes(value, 0, 1).astype(jnp.bfloat16)
-        for n in range(4):
-            blk[g * 4 + n] = value[:, :, n * 128:(n + 1) * 128]
+        wait(raw.at[g, mine], q_own.at[g])
+        wait(raw.at[g, pl.ds(0, 3)], q_rsem.at[g])
+        value = raw[g].astype(jnp.float32).reshape(32, blocks, 256)
+        turn[...] = jnp.swapaxes(value, 0, 1).astype(jnp.bfloat16)
+        for j in range(blocks):
+            value = turn[doc_block[j]]
+            blk[g * 2, j] = value[:, 0:128]
+            blk[g * 2 + 1, j] = value[:, 128:256]
 
     def wait_kv(v):
         for h in range(2):
             @pl.when(v == h * (STEPS // 2))
             def _():
-                own[GROUPS + h].wait()
+                wait(kv.at[h, mine], kv_own.at[h])
                 wait(kv.at[h, pl.ds(0, 3)], kv_rsem.at[h])
 
     sub = lax.broadcasted_iota(jnp.int32, (8, 128), 0)
@@ -416,7 +405,9 @@
         lse[v] = tile
 
     def finish(u, values):
-        value = jnp.stack([x.astype(jnp.float32) for x in values], axis=0)
+        for j in range(blocks):
+            done[j] = values[j]
+        value = jnp.stack([done[doc_ids[b]].astype(jnp.float32) for b in range(blocks)], axis=0)
         fin[u] = jnp.swapaxes(value, 0, 1).astype(jnp.bfloat16)
         column = pl.ds(pl.multiple_of(mine * 2048 + u * 128, 128), 128)
         for k in range(1, 4):
@@ -428,28 +419,29 @@
     def _():
         def pass_on(g):
             prepare(g)
-            for n in range(4):
-                c = g * 4 + n
+            for n in range(2):
+                c = g * 2 + n
                 remote(blk.at[c], s1r.at[c], s_ssem, s_rsem.at[c], away)
 
-        pass_on(0)
-        has_own = [has(b, first) for b in range(blocks)]
-        last_own = [last(b, first) for b in range(blocks)]
-        seam_last = last_at(seam_block, first)
+        for g in range(AHEAD):
+            pass_on(g)
+        has_own = [has(j, first) for j in range(blocks)]
+        last_own = [last(j, first) for j in range(blocks)]
+        seam_last = last_at(seam_doc, first)
 
         @pl.loop(0, STEPS + LAG + 1)
         def _(t):
-            @pl.when((t % 4 == 0) & (t < STEPS - 4))
-            def _():
-                pass_on(t // 4 + 1)
-
             @pl.when(t < STEPS)
             def _():
                 wait_kv(t)
                 wait(cr.at[t], c_rsem.at[t])
-                attend(t, lambda p: jnp.concatenate([blk[t, page_block[p]], cr[t, p]], axis=0))
+                attend(t, lambda p: jnp.concatenate([blk[t, page_doc[p]], cr[t, p]], axis=0))
                 remote(run.at[t, :, pl.ds(32, 96)], dr.at[t], d_ssem, d_rsem.at[t], away)
                 remote(lse.at[t], dlr.at[t], dl_ssem, dl_rsem.at[t], away)
+
+            @pl.when((t % 2 == 0) & (t < (GROUPS - AHEAD) * 2))
+            def _():
+                pass_on(t // 2 + AHEAD)
 
             @pl.when(t >= LAG + 1)
             def _():
@@ -458,14 +450,12 @@
                 wait(flr.at[u], fl_rsem.at[u])
                 near = to_col(pick([lse[u, p:p + 1] for p in range(4)], seam_last), 0, 32)
                 far = to_col(flr[u, 0:1], 0, 32)
-                whole = merge(
-                    run[u, seam_last, 0:32], near,
-                    of([fr[u, b] for b in range(blocks)], seam_block), far,
-                )
+                theirs = [fr[u, j] for j in range(blocks)]
+                whole = merge(run[u, seam_last, 0:32], near, pick(theirs, seam_doc), far)
                 values = []
-                for b in range(blocks):
-                    value = jnp.where(has_own[b], run[u, last_own[b], 0:32], fr[u, b])
-                    values.append(jnp.where(seam_cut & (seam_block == b), whole, value))
+                for j in range(blocks):
+                    value = jnp.where(has_own[j], run[u, last_own[j], 0:32], theirs[j])
+                    values.append(jnp.where(seam_cut & (seam_doc == j), whole, value))
                 finish(u, values)
 
         wait(blk, s_ssem)
@@ -474,21 +464,19 @@
 
     @pl.when(hub)
     def _():
-        prepare(jnp.int32(0))
-        has_rim = [has(b, rim) for b in range(blocks)]
         last_rim = [last(b, rim) for b in range(blocks)]
         has_own = [has(b, first) for b in range(blocks)]
         last_own = [last(b, first) for b in range(blocks)]
-        rim_block = [block_at(rim + p) for p in range(4)]
-        seam_rim, seam_own = last_at(seam_block, rim), last_at(seam_block, first)
-        mid_rim, mid_own = last_at(mid_block, rim), last_at(mid_block, first)
-        mid_has_rim = has_at(mid_block, rim)
+        rim_doc = [doc_at(rim + p) for p in range(4)]
+        seam_rim, seam_own = last_at(seam_doc, rim), last_at(seam_doc, first)
+        mid_rim, mid_own = last_at(mid_doc, rim), last_at(mid_doc, first)
+        mid_has_rim = has_at(mid_doc, rim)
         lane = lax.broadcasted_iota(jnp.int32, (1, 128), 1)
 
         def rows(ref, u):
             return [ref[u, p:p + 1] for p in range(4)]
 
-        @pl.loop(0, rounds + 1)
+        @pl.loop(0, rounds + BACK)
         def _(t):
             @pl.when((t >= LAG) & (t < rounds))
             def _():
@@ -502,7 +490,7 @@
                 )
                 for b in range(blocks):
                     value = jnp.where(has_own[b], run[w, last_own[b], 32:128], pick(rim_o, last_rim[b]))
-                    oh[w, b] = jnp.where(seam_cut & (seam_block == b), whole, value)
+                    oh[w, b] = jnp.where(seam_cut & (seam_doc == b), whole, value)
                 near = pick(rows(lse, w), mid_own)
                 far = jnp.where(mid_has_rim, pick(rows(dlr, w), mid_rim), FAR)
                 lh[w] = jnp.broadcast_to(join(near, far), (8, 128))
@@ -512,9 +500,9 @@
                 w = jnp.maximum(t - LAG, 0)
                 c = jnp.minimum(t, STEPS - 1)
 
-                @pl.when((t % 4 == 0) & (t > 0) & (t < STEPS))
-                def _():
-                    prepare(t // 4)
+                @pl.when((t % 2 == 0) & (t < STEPS))
+                def _():
+                    prepare(t // 2)
 
                 @pl.when(t < STEPS)
                 def _():
@@ -525,16 +513,38 @@
                     ask = other[b] & asks
                     xs[t, b, 0:32] = jnp.where(ask, s1r[c, b], oh[w, b, 32:64])
                     xs[t, b, 32:64] = jnp.where(ask, blk[c, b], oh[w, b, 64:96])
-                xs[t, blocks] = oh[w, mid_block, 32:96]
-                xls[t] = lh[w]
-                remote(xs.at[t], xr.at[t], x_ssem, x_rsem.at[t], across)
-                remote(xls.at[t], xlr.at[t], xl_ssem, xl_rsem.at[t], across)
-
-            @pl.when(t >= 1)
-            def _():
-                v = t - 1
-                wait(xr.at[v], x_rsem.at[v])
-                wait(xlr.at[v], xl_rsem.at[v])
+                @pl.when(t < LAG)
+                def _():
+                    part = pl.ds(1 - upper, blocks - 1)
+                    remote(xs.at[t, part], xr.at[t, part], x_ssem, x_rsem.at[t], across)
+
+                @pl.when((t >= LAG) & asks)
+                def _():
+                    xs[t, blocks] = oh[w, mid_doc, 32:96]
+                    remote(xs.at[t], xr.at[t], x_ssem, x_rsem.at[t], across)
+
+                @pl.when(t >= STEPS)
+                def _():
+                    part = pl.ds(upper, blocks - 1)
+                    remote(xs.at[t, part], xr.at[t, part], x_ssem, x_rsem.at[t], across)
+
+                @pl.when(t >= LAG)
+                def _():
+                    xls[t] = lh[w]
+                    remote(xls.at[t], xlr.at[t], xl_ssem, xl_rsem.at[t], across)
+
+            @pl.when(t >= BACK)
+            def _():
+                v = t - BACK
+                inner = (v >= LAG) & (v < STEPS)
+
+                @pl.when(inner)
+                def _():
+                    wait(xr.at[v], x_rsem.at[v])
+
+                @pl.when(jnp.logical_not(inner))
+                def _():
+                    wait(xr.at[v, pl.ds(0, blocks - 1)], x_rsem.at[v])
 
                 @pl.when(v < STEPS)
                 def _():
@@ -543,25 +553,28 @@
                         qt[v, b, 32:64] = blk[v, b]
                         qt[v, b, 64:128] = xr[v, b]
                     for p in range(4):
-                        cs[v, p] = qt[v, rim_block[p], 32:128]
+                        cs[v, p] = qt[v, rim_doc[p], 32:128]
                     remote(cs.at[v], cr.at[v], c_ssem, c_rsem.at[v], away)
 
                 @pl.when(v >= LAG)
                 def _():
                     u = v - LAG
+                    wait(xlr.at[v], xl_rsem.at[v])
                     near = jnp.where(lane < 32, pick(rows(lse, u), mid_own), lh[u, 0:1])
                     far = pltpu.roll(xlr[v, 0:1], 64, 1)
-                    part = jnp.concatenate([run[u, mid_own, 0:32], oh[u, mid_block, 0:32]], axis=0)
-                    whole = merge(part, to_col(near, 0, 64), xr[v, blocks], to_col(far, 0, 64))
+                    part = jnp.concatenate([run[u, mid_own, 0:32], oh[u, mid_doc, 0:32]], axis=0)
+                    theirs = pick([xr[v, j] for j in range(blocks)], mid_doc)
+                    theirs = jnp.where(v < STEPS, xr[v, blocks], theirs)
+                    whole = merge(part, to_col(near, 0, 64), theirs, to_col(far, 0, 64))
                     values = []
                     for b in range(blocks):
-                        cut = mid_cut & (mid_block == b)
+                        cut = mid_cut & (mid_doc == b)
                         leafs = jnp.where(other[b], xr[v, b, 0:32], run[u, last_own[b], 0:32])
                         hubs = jnp.where(other[b], xr[v, b, 32:64], oh[u, b, 0:32])
                         fs[u, b] = jnp.where(cut, whole[0:32], leafs)
                         values.append(jnp.where(cut, whole[32:64], hubs))
                     tail = pick(rows(lse, u), seam_own)
-                    tail = jnp.where(mid_cut & (mid_block == seam_block), join(tail, far), tail)
+                    tail = jnp.where(mid_cut & (mid_doc == seam_doc), join(tail, far), tail)
                     fls[u] = jnp.broadcast_to(tail, (8, 128))
                     remote(fs.at[u], fr.at[u], f_ssem, f_rsem.at[u], away)
                     remote(fls.at[u], flr.at[u], fl_ssem, fl_rsem.at[u], away)
@@ -571,10 +584,12 @@
             def _():
                 v = t - LAG + 1
                 wait_kv(v)
-                attend(v, lambda p: qt[v, page_block[p]])
-
-        wait(xs, x_ssem)
-        wait(xls, xl_ssem)
+                attend(v, lambda p: qt[v, page_doc[p]])
+
+        wait(xs.at[pl.ds(LAG, STEPS - LAG)], x_ssem)
+        for t in range(0, rounds, STEPS):
+            wait(xs.at[pl.ds(t, LAG), pl.ds(0, blocks - 1)], x_ssem)
+        wait(xls.at[pl.ds(LAG, STEPS)], xl_ssem)
         wait(cs, c_ssem)
         wait(fs, f_ssem)
         wait(fls, fl_ssem)
@@ -608,7 +623,7 @@
         in_specs=[smem_spec, smem_spec, any_spec, any_spec],
         out_specs=any_spec,
         scratch_shapes=[
-            pltpu.VMEM((GROUPS, 4, 8, blocks, 512), bf16),
+            pltpu.VMEM((GROUPS, 4, 8, blocks, 256), bf16),
             pltpu.VMEM((2, 4, 2, 512, 128), bf16),
             pieces, pieces, swaps, swaps, mids, mids,
             quads, quads, quads, tiles, pieces, pieces, tiles, tiles,
@@ -618,6 +633,8 @@
             pltpu.VMEM((STEPS, blocks, 96, 128), bf16),
             tiles,
             pltpu.VMEM((STEPS, 32, blocks, 128), bf16),
+            pltpu.VMEM((blocks, 32, 256), bf16),
+            pltpu.VMEM((blocks, 32, 128), bf16),
             pltpu.SMEM((blocks,), jnp.int32),
             one, dma((GROUPS,)), dma((GROUPS,)), one, dma((2,)), dma((2,)),
             one, step, one, mid, one, mid,

time: 110 us -> 92.7 us (0.84)
  Pallas kernels: 107 us -> 90.3 us
    pallas_call x1, Pallas kernels: 107 us -> 90.3 us  [line_call(): pl.pallas_call(line_kernel, out_shape=jax.ShapeDtypeStruct(queries.shape,...]
where the time goes in v2:
time: 92.7 us; the launch traced here: 92.5 us
  Pallas kernels  90.3 us (97%)
  local copies, waits for them, and re-layouts  2.26 us (2%)
    pallas_call x1, Pallas kernels, line_call(): pl.pallas_call(line_kernel, out_shape=jax.ShapeDtypeStruct(queries.shape,...  90.3 us
    unnamed x1, local copies, waits for them, and re-layouts  2.26 us

profile of v2, /device:TPU:0, one launch (start us, length us, event | category | flops | bytes accessed | tf_op | source)
XLA Modules:
  0.0 92.5 jit_solution(17394417365650214307)
XLA Ops:
  0.0 90.3 %shard_map.46 = bf16[8,8,8192]{2,1,0:T(8,128)(2,1)} custom-call(s32[8]{0:T(128)} %counts.1, s32[8]{0:T(128)} %doc_ids.1, bf16[8,8,8192]{2,1,0:T(8,128)(2,1)} %q_hbm.1, bf16[1,2,512,1024]{3,2,1,0:T(8,128)(2,1)} %kv_hbm.1), custom_call_target="tpu_custom_call" | custom-call | tf_op jit(solution)/shard_map/pallas_call | solution.py:620
  90.3 2.3 %copy.6 = bf16[8,8,8192]{2,1,0:T(8,128)(2,1)} copy(bf16[8,8,8192]{2,1,0:T(8,128)(2,1)} %shard_map.46) | data formatting | bytes 2097152

commit v3 on v2

--- a/solution.py
+++ b/solution.py
@@ -204,10 +204,10 @@
 
 
 STEPS = 16
-LAG = 6
+LAG = 7
 BACK = 2
-GROUPS = 8
-AHEAD = 4
+GROUPS = 16
+AHEAD = 8
 FAR = -1e30
 
 
@@ -274,7 +274,7 @@
         pl.semaphore_signal(barrier, inc=1, device_id={"ctx": across}, device_id_type=mesh_id)
 
     def lanes(i, g):
-        return pl.ds(pl.multiple_of(i * 2048 + g * 256, 128), 256)
+        return pl.ds(pl.multiple_of(i * 2048 + g * 128, 128), 128)
 
     def heads(i, h):
         return pl.ds(pl.multiple_of(i * 256 + h * 128, 128), 128)
@@ -363,12 +363,10 @@
     def prepare(g):
         wait(raw.at[g, mine], q_own.at[g])
         wait(raw.at[g, pl.ds(0, 3)], q_rsem.at[g])
-        value = raw[g].astype(jnp.float32).reshape(32, blocks, 256)
+        value = raw[g].astype(jnp.float32).reshape(32, blocks, 128)
         turn[...] = jnp.swapaxes(value, 0, 1).astype(jnp.bfloat16)
         for j in range(blocks):
-            value = turn[doc_block[j]]
-            blk[g * 2, j] = value[:, 0:128]
-            blk[g * 2 + 1, j] = value[:, 128:256]
+            blk[g, j] = turn[doc_block[j]]
 
     def wait_kv(v):
         for h in range(2):
@@ -419,9 +417,7 @@
     def _():
         def pass_on(g):
             prepare(g)
-            for n in range(2):
-                c = g * 2 + n
-                remote(blk.at[c], s1r.at[c], s_ssem, s_rsem.at[c], away)
+            remote(blk.at[g], s1r.at[g], s_ssem, s_rsem.at[g], away)
 
         for g in range(AHEAD):
             pass_on(g)
@@ -439,9 +435,9 @@
                 remote(run.at[t, :, pl.ds(32, 96)], dr.at[t], d_ssem, d_rsem.at[t], away)
                 remote(lse.at[t], dlr.at[t], dl_ssem, dl_rsem.at[t], away)
 
-            @pl.when((t % 2 == 0) & (t < (GROUPS - AHEAD) * 2))
-            def _():
-                pass_on(t // 2 + AHEAD)
+            @pl.when(t < GROUPS - AHEAD)
+            def _():
+                pass_on(t + AHEAD)
 
             @pl.when(t >= LAG + 1)
             def _():
@@ -500,9 +496,9 @@
                 w = jnp.maximum(t - LAG, 0)
                 c = jnp.minimum(t, STEPS - 1)
 
-                @pl.when((t % 2 == 0) & (t < STEPS))
-                def _():
-                    prepare(t // 2)
+                @pl.when(t < STEPS)
+                def _():
+                    prepare(t)
 
                 @pl.when(t < STEPS)
                 def _():
@@ -623,7 +619,7 @@
         in_specs=[smem_spec, smem_spec, any_spec, any_spec],
         out_specs=any_spec,
         scratch_shapes=[
-            pltpu.VMEM((GROUPS, 4, 8, blocks, 256), bf16),
+            pltpu.VMEM((GROUPS, 4, 8, blocks, 128), bf16),
             pltpu.VMEM((2, 4, 2, 512, 128), bf16),
             pieces, pieces, swaps, swaps, mids, mids,
             quads, quads, quads, tiles, pieces, pieces, tiles, tiles,
@@ -633,7 +629,7 @@
             pltpu.VMEM((STEPS, blocks, 96, 128), bf16),
             tiles,
             pltpu.VMEM((STEPS, 32, blocks, 128), bf16),
-            pltpu.VMEM((blocks, 32, 256), bf16),
+            pltpu.VMEM((blocks, 32, 128), bf16),
             pltpu.VMEM((blocks, 32, 128), bf16),
             pltpu.SMEM((blocks,), jnp.int32),
             one, dma((GROUPS,)), dma((GROUPS,)), one, dma((2,)), dma((2,)),

time: 92.7 us -> 90.7 us (0.978)
  Pallas kernels: 90.3 us -> 88.2 us
    pallas_call x1, Pallas kernels: 90.3 us -> 88.2 us  [line_call(): pl.pallas_call(line_kernel, out_shape=jax.ShapeDtypeStruct(queries.shape,...]
where the time goes in v3:
time: 90.7 us; the launch traced here: 90.5 us
  Pallas kernels  88.2 us (97%)
  local copies, waits for them, and re-layouts  2.26 us (2%)
    pallas_call x1, Pallas kernels, line_call(): pl.pallas_call(line_kernel, out_shape=jax.ShapeDtypeStruct(queries.shape,...  88.2 us
    unnamed x1, local copies, waits for them, and re-layouts  2.26 us

profile of v3, /device:TPU:0, one launch (start us, length us, event | category | flops | bytes accessed | tf_op | source)
XLA Modules:
  0.0 90.5 jit_solution(7857516762489084418)
XLA Ops:
  0.0 88.2 %shard_map.46 = bf16[8,8,8192]{2,1,0:T(8,128)(2,1)} custom-call(s32[8]{0:T(128)} %counts.1, s32[8]{0:T(128)} %doc_ids.1, bf16[8,8,8192]{2,1,0:T(8,128)(2,1)} %q_hbm.1, bf16[1,2,512,1024]{3,2,1,0:T(8,128)(2,1)} %kv_hbm.1), custom_call_target="tpu_custom_call" | custom-call | tf_op jit(solution)/shard_map/pallas_call | solution.py:616
  88.2 2.3 %copy.6 = bf16[8,8,8192]{2,1,0:T(8,128)(2,1)} copy(bf16[8,8,8192]{2,1,0:T(8,128)(2,1)} %shard_map.46) | data formatting | bytes 2097152
